TPU v7x, 32 devices: a whole 2x2x4 slice. The times are simulated.
32 devices in a mesh: sta: 4 (over y, x), evt: 8 (over z, core).
Axes of the slice: x: 2, y: 2, z: 4, core: 2. Of those that a mesh axis runs over, the one named last changes fastest.
Arguments:
- traces: bfloat16 [3, 32, 512, 2048], P(None, 'sta', 'evt'), may hold values from -96 to 96
- baz_bin: int32 [32, 512], P('sta', 'evt'), may hold values from 0 to 35
- inc_bin: int32 [32, 512], P('sta', 'evt'), may hold values from 0 to 7
- counts: int32 [32], P('sta'), may hold values from 64 to 512
- depth_index: int32 [32, 512], P('sta'), may hold values from 0 to 2046
- tile_of: int32 [32], replicated, may hold values from 0 to 15
Outputs:
- stack: float32 [16, 5, 2, 512], P('sta', None, None, 'evt')
All inputs are finite; a program needn't handle non-finite values.
Results may differ from a plain program's by a relative error of at most 0.0003.
Values sent between devices are 32-bit elements; how exact they have to be, the bound alone decides.
A program may use at most 64 MiB of HBM per device.

v0:
```python
import jax
import jax.numpy as jnp
from jax import lax
from jax.sharding import PartitionSpec as P

NS = 2048
DEPTHS = 512
BAZ_BINS = 36
TILE_DEV = 4


def solve_blocks(normal, right):
    factor = jnp.linalg.cholesky(normal)
    middle = jax.scipy.linalg.solve_triangular(factor, right, lower=True)
    return jax.scipy.linalg.solve_triangular(factor, middle, lower=True, trans=1)


def to_depths(values, indices):
    picks = indices[:, None, None, :]
    first = jnp.take_along_axis(values, picks, axis=3)
    second = jnp.take_along_axis(values, picks + 1, axis=3)
    return 0.5 * (first + second)


def body(traces, baz_bin, inc_bin, counts, depth_index, tile_of):
    highest = lax.Precision.HIGHEST
    stations = traces.shape[1]
    slots = traces.shape[2]
    evt_count = lax.axis_size("evt")
    depth_share = DEPTHS // evt_count
    phi = (baz_bin.astype(jnp.float32) + 0.5) * (2.0 * jnp.pi / BAZ_BINS)
    incidence = (12.0 + 2.5 * (inc_bin.astype(jnp.float32) + 0.5)) * (jnp.pi / 180.0)
    cosine = jnp.cos(phi)[:, :, None]
    sine = jnp.sin(phi)[:, :, None]
    vertical = traces[0].astype(jnp.float32)
    north = traces[1].astype(jnp.float32)
    east = traces[2].astype(jnp.float32)
    radial = -(cosine * north + sine * east)
    quality = jnp.cos(incidence)[:, :, None] * radial + jnp.sin(incidence)[:, :, None] * vertical
    transverse = sine * north - cosine * east
    data = jnp.concatenate([quality, transverse], axis=2)
    slot_ids = lax.axis_index("evt") * slots + jnp.arange(slots)
    live = (slot_ids[None, :] < counts[:, None]).astype(jnp.float32)
    harm = jnp.stack(
        [jnp.ones_like(phi), jnp.cos(phi), jnp.sin(phi), jnp.cos(2.0 * phi), jnp.sin(2.0 * phi)],
        axis=2,
    )
    weighted = harm * live[:, :, None]
    normal_part = jnp.einsum("sek,sel->skl", weighted, harm, precision=highest)
    rhs_part = jnp.einsum("sek,sec->skc", weighted, data, precision=highest)
    normal = lax.psum(normal_part, "evt") + jnp.eye(5, dtype=jnp.float32)[None]
    shares = lax.psum_scatter(rhs_part, "evt", scatter_dimension=2, tiled=True)
    solved = solve_blocks(normal, shares)
    coeff = lax.all_gather(solved, "evt", axis=2, tiled=True).reshape(stations, 5, 2, NS)
    mine = lax.dynamic_slice_in_dim(
        depth_index, lax.axis_index("evt") * depth_share, depth_share, 1
    )
    profile = to_depths(coeff, mine)
    first_tile = lax.axis_index("sta") * TILE_DEV
    own_tiles = first_tile + jnp.arange(TILE_DEV)
    members = jnp.sum((tile_of[None, :] == own_tiles[:, None]).astype(jnp.float32), axis=1)
    everyone = lax.all_gather(profile, "sta", axis=0, tiled=True)
    onehot = (tile_of[None, :] == own_tiles[:, None]).astype(jnp.float32)
    sums = jnp.einsum("ts,skcz->tkcz", onehot, everyone, precision=highest)
    return sums / jnp.maximum(members, 1.0)[:, None, None, None]


def solution(mesh):
    return jax.shard_map(
        body,
        mesh=mesh,
        in_specs=(
            P(None, "sta", "evt", None),
            P("sta", "evt"),
            P("sta", "evt"),
            P("sta"),
            P("sta", None),
            P(),
        ),
        out_specs=P("sta", None, None, "evt"),
        check_vma=False,
    )
```

profile of v0, /device:TPU:0, one launch (start us, length us, event | category | flops | bytes accessed | tf_op | source)
XLA Modules:
  0.0 130.2 jit_solution(14801742810654873437)
XLA Ops:
  6.5 0.8 fusion.24
  7.3 0.7 compare_convert_fusion
  8.0 6.8 %fusion.7 = (f32[8,64,2048]{2,1,0:T(8,128)}, f32[8,64,2048]{2,1,0:T(8,128)}) fusion(bf16[3,8,64,2048]{3,2,1,0:T(8,128)(2,1)} %param.8, f32[8,64]{1,0:T(8,128)S(1)} %get-tuple-element.18, f32[8,64]{1,0:T(8,128)S(1)} %get-tuple-element.13, f32[8,64]{1,0:T(8,128)S(1)} %get-tuple-element.15, f32[8,64]{1,0:T(8,128)S(1)} %get-tuple-element.19), kind=kLoop, calls=%fused_computation.13 | loop fusion | flops 13631488 | bytes 14688256 | tf_op jit(solution)/shard_map/add | solution.py:39
  14.9 0.0 copy-start.1
  14.9 7.3 %fusion = f32[8,5,4096]{2,1,0:T(8,128)} fusion(f32[8,64,2048]{2,1,0:T(8,128)} %get-tuple-element.7, f32[8,64,2048]{2,1,0:T(8,128)} %get-tuple-element.6, f32[8,64,5]{1,2,0:T(8,128)S(1)} %stack.19, f32[8,64]{1,0:T(8,128)S(1)} %compare_convert_fusion), kind=kOutput, calls=%fused_computation.2 | convolution fusion | flops 127928832 | bytes 9056256 | tf_op jit(solution)/shard_map/sek,sec->skc/dot_general | solution.py:50
  22.2 0.0 reduce-scatter.2.cloned.1.call-update
  22.2 0.2 fusion.10
  22.4 30.3 %psum.7 = f32[8,5,5]{1,2,0:T(8,128)S(1)} all-reduce(f32[8,5,5]{1,2,0:T(8,128)S(1)} %fusion.10), channel_id=1, replica_groups=mesh['sta'=4,'evt'=8] {'evt'}, use_global_device_ids=true, to_apply=%region_0.0 | all-reduce | flops 200 | bytes 1600 | tf_op jit(solution)/shard_map/psum | solution.py:51
  52.8 0.1 copy.30
  52.9 0.1 copy.31
  53.0 3.7 %custom-call.11 = f32[8,5,5]{2,1,0:T(8,128)S(1)} custom-call(f32[8,5,5]{2,1,0:T(8,128)S(1)} %fusion.17), custom_call_target="Cholesky" | custom-call | tf_op jit(solution)/shard_map/jit(cholesky)/cholesky | solution.py:13
  56.7 0.1 compare_reduce_fusion
  56.9 0.1 select_bitcast_fusion
  56.9 3.2 %custom-call.12 = f32[8,1,5,5]{2,3,1,0:T(8,128)S(1)} custom-call(f32[8,1,5,5]{3,2,1,0:T(8,128)S(1)} %select_bitcast_fusion), custom_call_target="InvertDiagBlocksLowerTriangular" | custom-call | tf_op jit(solution)/shard_map/jit(_solve_triangular)/vmap()/triangular_solve | solution.py:15
  60.1 0.1 bitcast_or_fusion.1
  60.2 0.1 reshape.123
  60.3 0.1 reshape.128
  60.4 0.1 and_bitcast_fusion.1
  60.5 0.2 fusion.28
  60.7 0.0 reduce-scatter.2.cloned.1.call-done
  60.7 1.2 fusion.15
  61.9 0.3 fusion.13
  62.2 16.4 %all_gather.6 = f32[8,5,4096]{2,1,0:T(8,128)S(1)} all-gather(f32[8,5,512]{2,1,0:T(8,128)S(1)} %fusion.13), channel_id=1, replica_groups=mesh['sta'=4,'evt'=8] {'evt'}, dimensions={2}, use_global_device_ids=true | all-gather | bytes 737280 | tf_op jit(solution)/shard_map/all_gather | solution.py:54
  78.5 0.6 reshape.133
  79.1 17.0 %copy.34 = f32[8,5,2,2048]{1,2,3,0:T(2,128)} copy(f32[8,5,2,2048]{3,2,1,0:T(2,128)S(1)} %reshape.133) | data formatting | bytes 1310720 | tf_op jit(solution)/shard_map/reshape | solution.py:54
  96.1 8.3 %gather_fusion = f32[512,5,2]{1,2,0:T(2,128)S(1)} fusion(f32[8,5,2,2048]{1,2,3,0:T(2,128)} %copy.34, s32[512]{0:T(512)S(1)} %reshape.123), kind=kCustom, calls=%fused_computation.clone | custom fusion | bytes 45056 | tf_op jit(solution)/shard_map/jit(take_along_axis)/gather | solution.py:20
  104.4 0.2 copy.44
  104.6 8.3 %gather_fusion.1 = f32[512,5,2]{1,2,0:T(2,128)S(1)} fusion(f32[8,5,2,2048]{1,2,3,0:T(2,128)} %copy.34, s32[512]{0:T(512)S(1)} %reshape.128), kind=kCustom, calls=%fused_computation.1.clone | custom fusion | bytes 45056 | tf_op jit(solution)/shard_map/jit(take_along_axis)/gather | solution.py:21
  113.0 0.2 copy.46
  113.2 9.3 %all_gather.7 = f32[32,5,2,64]{3,0,2,1:T(8,128)S(1)} all-gather(f32[8,5,2,64]{3,0,2,1:T(8,128)S(1)} %fusion.12), channel_id=1, replica_groups=mesh['sta'=4,'evt'=8] {'sta'}, dimensions={0}, use_global_device_ids=true | all-gather | bytes 102400 | tf_op jit(solution)/shard_map/all_gather | solution.py:62
  122.5 0.2 convolution_divide_fusion
  122.8 0.6 copy.38
  (16 shorter events, 0.1 us)
Async XLA Ops:
  6.5 54.2 %reduce-scatter.2.cloned.1.call-start = ((), (), s32[]{:S(2)}) async-start(), calls=%async_computation.1 | async-start | bytes 1179648 | tf_op jit(solution)/shard_map/reduce_scatter | solution.py:52
  14.9 45.2 %copy-start = (s32[8,512]{1,0:T(8,128)S(1)}, s32[8,512]{1,0:T(8,128)}, u32[]{:S(2)}) copy-start(s32[8,512]{1,0:T(8,128)} %param.12) | copy-start | bytes 49156
  14.9 45.6 %copy-start.1 = (s32[32]{0:T(128)S(1)}, s32[32]{0:T(128)}, u32[]{:S(2)}) copy-start(s32[32]{0:T(128)} %param.13) | copy-start | bytes 388
Sparse Core Ops, SparseCore 0:
  22.3 35.4 reduce-scatter.1
where the time goes:
time: 131 us; the launch traced here: 130 us
  blocking collectives  56 us (43%)
  local copies, waits for them, and re-layouts  35.7 us (27%)
  other arithmetic  15.8 us (12%)
  between operations  13.5 us (10%)
  matrix products  9.13 us (7%)
    psum x1, blocking collectives, body(): normal = lax.psum(normal_part, 'evt') + jnp.eye(5, dtype=jnp.float32)[None]  30.3 us
    reshape x2, local copies, waits for them, and re-layouts, body(): lax.all_gather(solved, 'evt', axis=2, tiled=True)  17.5 us
    all_gather x1, blocking collectives, body(): lax.all_gather(solved, 'evt', axis=2, tiled=True)  16.4 us
    all_gather x1, blocking collectives, body(): everyone = lax.all_gather(profile, 'sta', axis=0, tiled=True)  9.33 us
    gather x3, local copies, waits for them, and re-layouts, to_depths(): second = jnp.take_along_axis(values, picks + 1, axis=3)  8.62 us
    gather x3, local copies, waits for them, and re-layouts, to_depths(): first = jnp.take_along_axis(values, picks, axis=3)  8.62 us
    dot_general x1, matrix products, body(): rhs_part = jnp.einsum('sek,sec->skc', weighted, data, precision=highest)  7.27 us
    add x1, other arithmetic, body(): jnp.cos(incidence)[:, :, None] * radial  6.81 us
  transfers between devices with their start and end apart: 1, of which 0 were waited for; matrix products, arithmetic and copies ran while one was open for 6% of the time, Pallas kernels for 0%

commit v1 on v0

v1 whole, which is shorter than its diff:
```python
import functools

import jax
import jax.numpy as jnp
from jax import lax
from jax.experimental import pallas as pl
from jax.experimental.pallas import tpu as pltpu
from jax.sharding import PartitionSpec as P

BAZ_BINS = 36
HARMS = 5
LANES = 128
ROWS = 8
USED = 6
HALF = LANES // 2


def pick_lanes(values, lanes):
    return jnp.take_along_axis(values, lanes, axis=1, mode="promise_in_bounds")


def kernel(
    evt_count,
    sta_count,
    tiles,
    traces_ref,
    baz_ref,
    inc_ref,
    counts_ref,
    depth_ref,
    tile_ref,
    out_ref,
    trace_buf,
    weight_buf,
    normal_buf,
    send_buf,
    recv_buf,
    sum_buf,
    fit_buf,
    fit_recv,
    load_sem,
    send_sem,
    recv_sem,
    fit_send_sem,
    fit_recv_sem,
):
    stations, slots = baz_ref.shape
    samples = traces_ref.shape[3]
    depths = depth_ref.shape[1]
    share = depths // evt_count
    evt = lax.axis_index("evt")
    sta = lax.axis_index("sta")
    f32 = jnp.float32

    def load(s):
        return pltpu.make_async_copy(traces_ref.at[:, s], trace_buf.at[s], load_sem.at[s])

    for s in range(stations):
        load(s).start()
    barrier = pltpu.get_barrier_semaphore()
    for j in range(1, evt_count):
        pl.semaphore_signal(
            barrier, inc=1, device_id={"evt": lax.rem(evt + j, evt_count)},
            device_id_type=pl.DeviceIdType.MESH,
        )
    for j in range(1, sta_count):
        pl.semaphore_signal(
            barrier, inc=1, device_id={"sta": lax.rem(sta + j, sta_count)},
            device_id_type=pl.DeviceIdType.MESH,
        )

    phi = (baz_ref[...].astype(f32) + 0.5) * (2.0 * jnp.pi / BAZ_BINS)
    tilt = (12.0 + 2.5 * (inc_ref[...].astype(f32) + 0.5)) * (jnp.pi / 180.0)
    cosine, sine = jnp.cos(phi), jnp.sin(phi)
    cos_tilt, sin_tilt = jnp.cos(tilt), jnp.sin(tilt)
    row_ids = lax.broadcasted_iota(jnp.int32, (stations, slots), 0)
    total = jnp.zeros((stations, slots), jnp.int32)
    for s in range(stations):
        total = jnp.where(row_ids == s, counts_ref[s], total)
    slot_ids = evt * slots + lax.broadcasted_iota(jnp.int32, (stations, slots), 1)
    live = jnp.where(slot_ids < total, 1.0, 0.0).astype(f32)
    harm = [
        jnp.ones_like(phi),
        cosine,
        sine,
        2.0 * cosine * cosine - 1.0,
        2.0 * sine * cosine,
    ]
    weighted = [h * live for h in harm]
    parts = [
        [sin_tilt, -cos_tilt * cosine, -cos_tilt * sine],
        [jnp.zeros_like(phi), sine, -cosine],
    ]
    weight_buf[...] = jnp.zeros_like(weight_buf)
    for c in range(2):
        for k in range(HARMS):
            for m in range(3):
                weight_buf[c * ROWS + k, :, m * slots:(m + 1) * slots] = weighted[k] * parts[c][m]
    lane_ids = lax.broadcasted_iota(jnp.int32, (stations, LANES), 1)
    packed = jnp.zeros((stations, LANES), f32)
    place = 0
    for k in range(HARMS):
        for l in range(k + 1):
            column = jnp.sum(weighted[k] * harm[l], axis=1, keepdims=True)
            packed = jnp.where(lane_ids == place, column, packed)
            place += 1
    normal_buf[...] = packed

    pl.semaphore_wait(barrier, evt_count - 1 + sta_count - 1)

    def remote(j, s):
        target = lax.rem(evt + j, evt_count)
        return pltpu.make_async_remote_copy(
            src_ref=send_buf.at[target, s, 0:USED],
            dst_ref=recv_buf.at[j - 1, s, 0:USED],
            send_sem=send_sem.at[j - 1],
            recv_sem=recv_sem.at[j - 1],
            device_id={"evt": target},
            device_id_type=pl.DeviceIdType.MESH,
        )

    lane8 = lax.broadcasted_iota(jnp.int32, (ROWS, LANES), 1)
    row8 = lax.broadcasted_iota(jnp.int32, (ROWS, LANES), 0)

    def station(s, carry):
        load(s).wait()
        weights = weight_buf[:, s, :]
        high = weights.astype(jnp.bfloat16)
        low = (weights - high.astype(f32)).astype(jnp.bfloat16)
        block = trace_buf[s].reshape(3 * slots, samples)
        right = jnp.dot(
            jnp.concatenate([high, low], axis=0), block, preferred_element_type=f32
        )
        pair = right[0:2 * ROWS] + right[2 * ROWS:4 * ROWS]
        pair = 0.5 * (pair + pltpu.roll(pair, samples - 1, 1))
        first, second = pair[0:ROWS], pair[ROWS:2 * ROWS]
        normal_row = jnp.broadcast_to(normal_buf[pl.ds(s, 1), :], (ROWS, LANES))
        picks = depth_ref[pl.ds(s, 1), :]
        for z in range(depths // LANES):
            index = jnp.broadcast_to(picks[:, z * LANES:(z + 1) * LANES], (ROWS, LANES))
            chunk = lax.shift_right_logical(index, 7)
            lane = lax.bitwise_and(index, LANES - 1)
            got = [jnp.zeros((ROWS, LANES), f32)] * 2
            for n in range(samples // LANES):
                here = chunk == n
                for c, values in enumerate((first, second)):
                    taken = pick_lanes(values[:, n * LANES:(n + 1) * LANES], lane)
                    got[c] = jnp.where(here, taken, got[c])
            for d in range(LANES // share):
                left = got[0] if d == 0 else pltpu.roll(got[0], LANES - d * share, 1)
                move = (HALF - d * share) % LANES
                rest = got[1] if move == 0 else pltpu.roll(got[1], move, 1)
                both = jnp.where(lane8 < HALF, left, rest)
                send_buf[z * (LANES // share) + d, s] = jnp.where(row8 == HARMS, normal_row, both)
        for j in range(1, evt_count):
            remote(j, s).start()
        return carry

    lax.fori_loop(0, stations, station, 0)

    def whole(j):
        return pltpu.make_async_remote_copy(
            src_ref=send_buf.at[lax.rem(evt + j, evt_count), :, 0:USED],
            dst_ref=recv_buf.at[j - 1, :, 0:USED],
            send_sem=send_sem.at[j - 1],
            recv_sem=recv_sem.at[j - 1],
            device_id={"evt": lax.rem(evt + j, evt_count)},
            device_id_type=pl.DeviceIdType.MESH,
        )

    sums = send_buf[evt, :, 0:USED]
    for j in range(1, evt_count):
        whole(j).wait_recv()
        sums = sums + recv_buf[j - 1, :, 0:USED]
    sum_buf[:, 0:USED] = sums

    right = [sum_buf[:, k, :] for k in range(HARMS)]
    entries = sum_buf[:, HARMS, :]
    matrix = {}
    place = 0
    for k in range(HARMS):
        for l in range(k + 1):
            value = jnp.broadcast_to(entries[:, place:place + 1], (stations, LANES))
            matrix[k, l] = value + 1.0 if k == l else value
            place += 1
    inverse = []
    for p in range(HARMS):
        inverse.append(1.0 / matrix[p, p])
        for k in range(p + 1, HARMS):
            ratio = matrix[k, p] * inverse[p]
            for l in range(p + 1, k + 1):
                matrix[k, l] = matrix[k, l] - ratio * matrix[l, p]
            right[k] = right[k] - ratio * right[p]
    solved = [None] * HARMS
    for k in reversed(range(HARMS)):
        value = right[k]
        for l in range(k + 1, HARMS):
            value = value - matrix[l, k] * solved[l]
        solved[k] = value * inverse[k]
        fit_buf[k] = solved[k]

    def fits(j):
        return pltpu.make_async_remote_copy(
            src_ref=fit_buf,
            dst_ref=fit_recv.at[j - 1],
            send_sem=fit_send_sem.at[j - 1],
            recv_sem=fit_recv_sem.at[j - 1],
            device_id={"sta": lax.rem(sta + j, sta_count)},
            device_id_type=pl.DeviceIdType.MESH,
        )

    for j in range(1, sta_count):
        fits(j).start()

    ids = lax.broadcasted_iota(jnp.int32, (stations, LANES), 0)
    masks = []
    for j in range(sta_count):
        base = lax.rem(sta + sta_count - j, sta_count) * stations
        of = jnp.zeros((stations, LANES), jnp.int32)
        for s in range(stations):
            of = jnp.where(ids == s, tile_ref[base + s], of)
        masks.append(
            [jnp.where(of == sta * tiles + t, 1.0, 0.0).astype(f32) for t in range(tiles)]
        )
    scale = []
    for t in range(tiles):
        members = functools.reduce(jnp.add, [m[t] for m in masks])
        scale.append(jnp.maximum(jnp.sum(members, axis=0, keepdims=True), 1.0))
    stack = [[masks[0][t] * solved[k] for k in range(HARMS)] for t in range(tiles)]
    for j in range(1, sta_count):
        fits(j).wait_recv()
        for k in range(HARMS):
            value = fit_recv[j - 1, k]
            for t in range(tiles):
                stack[t][k] = stack[t][k] + masks[j][t] * value
    for t in range(tiles):
        for k in range(HARMS):
            row = jnp.sum(stack[t][k], axis=0, keepdims=True) / scale[t]
            out_ref[t, k, 0:1, :] = row[:, 0:share]
            out_ref[t, k, 1:2, :] = row[:, HALF:HALF + share]
    for j in range(1, evt_count):
        whole(j).wait_send()
    for j in range(1, sta_count):
        fits(j).wait_send()


def body(evt_count, sta_count, traces, baz_bin, inc_bin, counts, depth_index, tile_of):
    _, stations, slots, samples = traces.shape
    depths = depth_index.shape[1]
    share = depths // evt_count
    tiles = tile_count(tile_of.shape[0]) // sta_count
    vmem = pl.BlockSpec(memory_space=pltpu.VMEM)
    smem = pl.BlockSpec(memory_space=pltpu.SMEM)
    f32 = jnp.float32
    return pl.pallas_call(
        functools.partial(kernel, evt_count, sta_count, tiles),
        out_shape=jax.ShapeDtypeStruct((tiles, HARMS, 2, share), f32),
        in_specs=[pl.BlockSpec(memory_space=pl.ANY), vmem, vmem, smem, vmem, smem],
        out_specs=vmem,
        scratch_shapes=[
            pltpu.VMEM((stations, 3, slots, samples), traces.dtype),
            pltpu.VMEM((2 * ROWS, stations, 3 * slots), f32),
            pltpu.VMEM((stations, LANES), f32),
            pltpu.VMEM((evt_count, stations, ROWS, LANES), f32),
            pltpu.VMEM((evt_count - 1, stations, ROWS, LANES), f32),
            pltpu.VMEM((stations, ROWS, LANES), f32),
            pltpu.VMEM((HARMS, stations, LANES), f32),
            pltpu.VMEM((sta_count - 1, HARMS, stations, LANES), f32),
            pltpu.SemaphoreType.DMA((stations,)),
            pltpu.SemaphoreType.DMA((evt_count - 1,)),
            pltpu.SemaphoreType.DMA((evt_count - 1,)),
            pltpu.SemaphoreType.DMA((sta_count - 1,)),
            pltpu.SemaphoreType.DMA((sta_count - 1,)),
        ],
        compiler_params=pltpu.CompilerParams(collective_id=0, has_side_effects=True),
    )(traces, baz_bin, inc_bin, counts, depth_index, tile_of)


def tile_count(stations):
    return stations // 2


def solution(mesh):
    return jax.shard_map(
        functools.partial(body, mesh.shape["evt"], mesh.shape["sta"]),
        mesh=mesh,
        in_specs=(
            P(None, "sta", "evt", None),
            P("sta", "evt"),
            P("sta", "evt"),
            P("sta"),
            P("sta", None),
            P(),
        ),
        out_specs=P("sta", None, None, "evt"),
        check_vma=False,
    )
```

time: 131 us -> 20.9 us (0.16)
  blocking collectives: 56 us -> 0 us
  local copies, waits for them, and re-layouts: 35.7 us -> 1.34 us
  Pallas kernels: 0 us -> 19.3 us
  other arithmetic: 15.8 us -> 0 us
  between operations: 13.5 us -> 0.01 us
  matrix products: 9.13 us -> 0 us
    psum x1 -> x0, blocking collectives: 30.3 us -> none  [body(): normal = lax.psum(normal_part, 'evt') + jnp.eye(5, dtype=jnp.float32)[None]]
    all_gather x2 -> x0, blocking collectives: 25.7 us -> none  [the longest x1 16.4 us: body(): lax.all_gather(solved, 'evt', axis=2, tiled=True)]
    pallas_call x0 -> x1, Pallas kernels: none -> 19.3 us  [body(): pl.pallas_call(functools.partial(kernel, evt_count, sta_count, tiles), ou...]
    reshape x2 -> x0, local copies, waits for them, and re-layouts: 17.5 us -> none  [body(): lax.all_gather(solved, 'evt', axis=2, tiled=True)]
    gather x6 -> x0, local copies, waits for them, and re-layouts: 17.2 us -> none  [the longest x3 8.62 us: to_depths(): second = jnp.take_along_axis(values, picks + 1, axis=3)]
    dot_general x3 -> x0, matrix products: 7.67 us -> none  [the longest x1 7.27 us: body(): rhs_part = jnp.einsum('sek,sec->skc', weighted, data, precision=highest)]
    another operation x7 -> x0, other arithmetic: 7.07 us -> none  [the longest x4 3.8 us: solve_blocks(): factor = jnp.linalg.cholesky(normal)]
    add x4 -> x0, other arithmetic: 6.82 us -> none  [the longest x1 6.81 us: body(): jnp.cos(incidence)[:, :, None] * radial]
  transfers between devices with their start and end apart: 1 -> 0, of which waited for: 0 -> 0; matrix products, arithmetic and copies ran while one was open for 6% -> 0% of each run, Pallas kernels for 0% -> 0%
where the time goes in v1:
time: 20.9 us; the launch traced here: 20.7 us
  Pallas kernels  19.3 us (92%)
  local copies, waits for them, and re-layouts  1.34 us (6%)
    pallas_call x1, Pallas kernels, body(): pl.pallas_call(functools.partial(kernel, evt_count, sta_count, tiles), ou...  19.3 us
    unnamed x1, local copies, waits for them, and re-layouts  1.34 us

profile of v1, /device:TPU:0, one launch (start us, length us, event | category | flops | bytes accessed | tf_op | source)
XLA Modules:
  0.0 20.7 jit_solution(319813221895203416)
XLA Ops:
  0.0 19.3 %shard_map.64 = f32[4,5,2,64]{3,2,1,0:T(2,128)} custom-call(bf16[3,8,64,2048]{3,2,1,0:T(8,128)(2,1)} %traces_ref.1, s32[8,64]{1,0:T(8,128)} %baz_ref.1, s32[8,64]{1,0:T(8,128)} %inc_ref.1, s32[8]{0:T(128)} %counts_ref.1, s32[8,512]{1,0:T(8,128)} %depth_ref.1, s32[32]{0:T(128)} %tile_ref.1), custom_call_target="tpu_custom_call" | custom-call | tf_op jit(solution)/shard_map/pallas_call | solution.py:255
  19.4 1.3 %copy.8 = f32[4,5,2,64]{3,2,1,0:T(2,128)} copy(f32[4,5,2,64]{3,2,1,0:T(2,128)} %shard_map.64) | data formatting | bytes 20480

commit v2 on v1

--- a/solution.py
+++ b/solution.py
@@ -13,6 +13,7 @@
 ROWS = 8
 USED = 6
 HALF = LANES // 2
+GROUP = 2
 
 
 def pick_lanes(values, lanes):
@@ -24,13 +25,18 @@
     sta_count,
     tiles,
     traces_ref,
+    baz_hbm,
+    inc_hbm,
+    counts_hbm,
+    depth_hbm,
+    tile_hbm,
+    out_ref,
+    trace_buf,
     baz_ref,
     inc_ref,
     counts_ref,
     depth_ref,
     tile_ref,
-    out_ref,
-    trace_buf,
     weight_buf,
     normal_buf,
     send_buf,
@@ -39,6 +45,7 @@
     fit_buf,
     fit_recv,
     load_sem,
+    small_sem,
     send_sem,
     recv_sem,
     fit_send_sem,
@@ -55,6 +62,20 @@
     def load(s):
         return pltpu.make_async_copy(traces_ref.at[:, s], trace_buf.at[s], load_sem.at[s])
 
+    small = [
+        pltpu.make_async_copy(src, dst, small_sem.at[n])
+        for n, (src, dst) in enumerate(
+            [
+                (baz_hbm, baz_ref),
+                (inc_hbm, inc_ref),
+                (counts_hbm, counts_ref),
+                (depth_hbm, depth_ref),
+                (tile_hbm, tile_ref),
+            ]
+        )
+    ]
+    for copy in small:
+        copy.start()
     for s in range(stations):
         load(s).start()
     barrier = pltpu.get_barrier_semaphore()
@@ -68,6 +89,9 @@
             barrier, inc=1, device_id={"sta": lax.rem(sta + j, sta_count)},
             device_id_type=pl.DeviceIdType.MESH,
         )
+
+    for copy in small:
+        copy.wait()
 
     phi = (baz_ref[...].astype(f32) + 0.5) * (2.0 * jnp.pi / BAZ_BINS)
     tilt = (12.0 + 2.5 * (inc_ref[...].astype(f32) + 0.5)) * (jnp.pi / 180.0)
@@ -106,13 +130,11 @@
             place += 1
     normal_buf[...] = packed
 
-    pl.semaphore_wait(barrier, evt_count - 1 + sta_count - 1)
-
     def remote(j, s):
         target = lax.rem(evt + j, evt_count)
         return pltpu.make_async_remote_copy(
-            src_ref=send_buf.at[target, s, 0:USED],
-            dst_ref=recv_buf.at[j - 1, s, 0:USED],
+            src_ref=send_buf.at[target, pl.ds(s, GROUP), 0:USED],
+            dst_ref=recv_buf.at[j - 1, pl.ds(s, GROUP), 0:USED],
             send_sem=send_sem.at[j - 1],
             recv_sem=recv_sem.at[j - 1],
             device_id={"evt": target},
@@ -122,8 +144,7 @@
     lane8 = lax.broadcasted_iota(jnp.int32, (ROWS, LANES), 1)
     row8 = lax.broadcasted_iota(jnp.int32, (ROWS, LANES), 0)
 
-    def station(s, carry):
-        load(s).wait()
+    def right_sides(s):
         weights = weight_buf[:, s, :]
         high = weights.astype(jnp.bfloat16)
         low = (weights - high.astype(f32)).astype(jnp.bfloat16)
@@ -132,7 +153,9 @@
             jnp.concatenate([high, low], axis=0), block, preferred_element_type=f32
         )
         pair = right[0:2 * ROWS] + right[2 * ROWS:4 * ROWS]
-        pair = 0.5 * (pair + pltpu.roll(pair, samples - 1, 1))
+        return 0.5 * (pair + pltpu.roll(pair, samples - 1, 1))
+
+    def pick(s, pair):
         first, second = pair[0:ROWS], pair[ROWS:2 * ROWS]
         normal_row = jnp.broadcast_to(normal_buf[pl.ds(s, 1), :], (ROWS, LANES))
         picks = depth_ref[pl.ds(s, 1), :]
@@ -152,11 +175,24 @@
                 rest = got[1] if move == 0 else pltpu.roll(got[1], move, 1)
                 both = jnp.where(lane8 < HALF, left, rest)
                 send_buf[z * (LANES // share) + d, s] = jnp.where(row8 == HARMS, normal_row, both)
+
+    def step(i, carry):
+        at = i * GROUP
+        for g in range(GROUP):
+            load(at + g).wait()
+        pairs = [right_sides(at + g) for g in range(GROUP)]
+        for g in range(GROUP):
+            pick(at + g, pairs[g])
+
+        @pl.when(i == 0)
+        def _():
+            pl.semaphore_wait(barrier, evt_count - 1 + sta_count - 1)
+
         for j in range(1, evt_count):
-            remote(j, s).start()
+            remote(j, at).start()
         return carry
 
-    lax.fori_loop(0, stations, station, 0)
+    lax.fori_loop(0, stations // GROUP, step, 0)
 
     def whole(j):
         return pltpu.make_async_remote_copy(
@@ -250,15 +286,20 @@
     share = depths // evt_count
     tiles = tile_count(tile_of.shape[0]) // sta_count
     vmem = pl.BlockSpec(memory_space=pltpu.VMEM)
-    smem = pl.BlockSpec(memory_space=pltpu.SMEM)
+    anywhere = pl.BlockSpec(memory_space=pl.ANY)
     f32 = jnp.float32
     return pl.pallas_call(
         functools.partial(kernel, evt_count, sta_count, tiles),
-        out_shape=jax.ShapeDtypeStruct((tiles, HARMS, 2, share), f32),
-        in_specs=[pl.BlockSpec(memory_space=pl.ANY), vmem, vmem, smem, vmem, smem],
+        out_shape=pltpu.VMEM((tiles, HARMS, 2, share), f32),
+        in_specs=[anywhere] * 6,
         out_specs=vmem,
         scratch_shapes=[
             pltpu.VMEM((stations, 3, slots, samples), traces.dtype),
+            pltpu.VMEM(baz_bin.shape, jnp.int32),
+            pltpu.VMEM(inc_bin.shape, jnp.int32),
+            pltpu.SMEM(counts.shape, jnp.int32),
+            pltpu.VMEM(depth_index.shape, jnp.int32),
+            pltpu.SMEM(tile_of.shape, jnp.int32),
             pltpu.VMEM((2 * ROWS, stations, 3 * slots), f32),
             pltpu.VMEM((stations, LANES), f32),
             pltpu.VMEM((evt_count, stations, ROWS, LANES), f32),
@@ -267,6 +308,7 @@
             pltpu.VMEM((HARMS, stations, LANES), f32),
             pltpu.VMEM((sta_count - 1, HARMS, stations, LANES), f32),
             pltpu.SemaphoreType.DMA((stations,)),
+            pltpu.SemaphoreType.DMA((5,)),
             pltpu.SemaphoreType.DMA((evt_count - 1,)),
             pltpu.SemaphoreType.DMA((evt_count - 1,)),
             pltpu.SemaphoreType.DMA((sta_count - 1,)),

time: 20.9 us -> 18.4 us (0.88)
  Pallas kernels: 19.3 us -> 17.7 us
  local copies, waits for them, and re-layouts: 1.34 us -> 0.61 us
    pallas_call x1, Pallas kernels: 19.3 us -> 17.7 us  [body(): pl.pallas_call(functools.partial(kernel, evt_count, sta_count, tiles), ou...]
    unnamed x1, local copies, waits for them, and re-layouts: 1.34 us -> 0.61 us
where the time goes in v2:
time: 18.4 us; the launch traced here: 18.3 us
  Pallas kernels  17.7 us (96%)
  local copies, waits for them, and re-layouts  0.61 us (3%)
    pallas_call x1, Pallas kernels, body(): pl.pallas_call(functools.partial(kernel, evt_count, sta_count, tiles), ou...  17.7 us
    unnamed x1, local copies, waits for them, and re-layouts  0.61 us

profile of v2, /device:TPU:0, one launch (start us, length us, event | category | flops | bytes accessed | tf_op | source)
XLA Modules:
  0.0 18.3 jit_solution(327098400705849821)
XLA Ops:
  0.0 17.7 %shard_map.64 = f32[4,5,2,64]{3,2,1,0:T(2,128)S(1)} custom-call(bf16[3,8,64,2048]{3,2,1,0:T(8,128)(2,1)} %traces_ref.1, s32[8,64]{1,0:T(8,128)} %baz_hbm.1, s32[8,64]{1,0:T(8,128)} %inc_hbm.1, s32[8]{0:T(128)} %counts_hbm.1, s32[8,512]{1,0:T(8,128)} %depth_hbm.1, s32[32]{0:T(128)} %tile_hbm.1), custom_call_target="tpu_custom_call" | custom-call | tf_op jit(solution)/shard_map/pallas_call | solution.py:291
  17.7 0.6 %copy.8 = f32[4,5,2,64]{3,2,1,0:T(2,128)} copy(f32[4,5,2,64]{3,2,1,0:T(2,128)S(1)} %shard_map.64) | data formatting | bytes 20480

commit v3 on v2

--- a/solution.py
+++ b/solution.py
@@ -11,7 +11,8 @@
 HARMS = 5
 LANES = 128
 ROWS = 8
-USED = 6
+USED = HARMS
+TERMS = 16
 HALF = LANES // 2
 GROUP = 2
 
@@ -38,7 +39,9 @@
     depth_ref,
     tile_ref,
     weight_buf,
+    left_buf,
     normal_buf,
+    normal_recv,
     send_buf,
     recv_buf,
     sum_buf,
@@ -48,6 +51,8 @@
     small_sem,
     send_sem,
     recv_sem,
+    normal_send_sem,
+    normal_recv_sem,
     fit_send_sem,
     fit_recv_sem,
 ):
@@ -118,17 +123,40 @@
     weight_buf[...] = jnp.zeros_like(weight_buf)
     for c in range(2):
         for k in range(HARMS):
+            at = (c * ROWS + k) * stations
             for m in range(3):
-                weight_buf[c * ROWS + k, :, m * slots:(m + 1) * slots] = weighted[k] * parts[c][m]
+                lane = m * slots
+                weight_buf[
+                    lane // LANES, at:at + stations, lane % LANES:lane % LANES + slots
+                ] = weighted[k] * parts[c][m]
+    for s in range(stations):
+        for n in range(weight_buf.shape[0]):
+            weights = weight_buf[n, pl.ds(s, 2 * ROWS, stride=stations), :]
+            high = weights.astype(jnp.bfloat16)
+            low = (weights - high.astype(f32)).astype(jnp.bfloat16)
+            left_buf[s, 0:2 * ROWS, n * LANES:(n + 1) * LANES] = high
+            left_buf[s, 2 * ROWS:4 * ROWS, n * LANES:(n + 1) * LANES] = low
     lane_ids = lax.broadcasted_iota(jnp.int32, (stations, LANES), 1)
+    station_ids = lax.broadcasted_iota(jnp.int32, (stations, LANES), 0)
     packed = jnp.zeros((stations, LANES), f32)
     place = 0
     for k in range(HARMS):
         for l in range(k + 1):
             column = jnp.sum(weighted[k] * harm[l], axis=1, keepdims=True)
-            packed = jnp.where(lane_ids == place, column, packed)
+            packed = jnp.where(lane_ids % TERMS == place, column, packed)
             place += 1
-    normal_buf[...] = packed
+    packed = jnp.where(lane_ids // TERMS == station_ids, packed, 0.0)
+    normal_buf[0:1] = jnp.sum(packed, axis=0, keepdims=True)
+
+    def normals(j):
+        return pltpu.make_async_remote_copy(
+            src_ref=normal_buf.at[0:1],
+            dst_ref=normal_recv.at[j - 1, 0:1],
+            send_sem=normal_send_sem.at[j - 1],
+            recv_sem=normal_recv_sem.at[j - 1],
+            device_id={"evt": lax.rem(evt + j, evt_count)},
+            device_id_type=pl.DeviceIdType.MESH,
+        )
 
     def remote(j, s):
         target = lax.rem(evt + j, evt_count)
@@ -142,22 +170,15 @@
         )
 
     lane8 = lax.broadcasted_iota(jnp.int32, (ROWS, LANES), 1)
-    row8 = lax.broadcasted_iota(jnp.int32, (ROWS, LANES), 0)
 
     def right_sides(s):
-        weights = weight_buf[:, s, :]
-        high = weights.astype(jnp.bfloat16)
-        low = (weights - high.astype(f32)).astype(jnp.bfloat16)
         block = trace_buf[s].reshape(3 * slots, samples)
-        right = jnp.dot(
-            jnp.concatenate([high, low], axis=0), block, preferred_element_type=f32
-        )
+        right = jnp.dot(left_buf[s, :, 0:3 * slots], block, preferred_element_type=f32)
         pair = right[0:2 * ROWS] + right[2 * ROWS:4 * ROWS]
         return 0.5 * (pair + pltpu.roll(pair, samples - 1, 1))
 
     def pick(s, pair):
         first, second = pair[0:ROWS], pair[ROWS:2 * ROWS]
-        normal_row = jnp.broadcast_to(normal_buf[pl.ds(s, 1), :], (ROWS, LANES))
         picks = depth_ref[pl.ds(s, 1), :]
         for z in range(depths // LANES):
             index = jnp.broadcast_to(picks[:, z * LANES:(z + 1) * LANES], (ROWS, LANES))
@@ -173,8 +194,7 @@
                 left = got[0] if d == 0 else pltpu.roll(got[0], LANES - d * share, 1)
                 move = (HALF - d * share) % LANES
                 rest = got[1] if move == 0 else pltpu.roll(got[1], move, 1)
-                both = jnp.where(lane8 < HALF, left, rest)
-                send_buf[z * (LANES // share) + d, s] = jnp.where(row8 == HARMS, normal_row, both)
+                send_buf[z * (LANES // share) + d, s] = jnp.where(lane8 < HALF, left, rest)
 
     def step(i, carry):
         at = i * GROUP
@@ -187,6 +207,8 @@
         @pl.when(i == 0)
         def _():
             pl.semaphore_wait(barrier, evt_count - 1 + sta_count - 1)
+            for j in range(1, evt_count):
+                normals(j).start()
 
         for j in range(1, evt_count):
             remote(j, at).start()
@@ -204,35 +226,46 @@
             device_id_type=pl.DeviceIdType.MESH,
         )
 
+    row = normal_buf[0:1]
+    for j in range(1, evt_count):
+        normals(j).wait_recv()
+        row = row + normal_recv[j - 1, 0:1]
+    entries = jnp.broadcast_to(row, (stations, LANES))
+    entries = jnp.where(lane_ids // TERMS == station_ids, entries, 0.0)
+    matrix = {}
+    place = 0
+    for k in range(HARMS):
+        for l in range(k + 1):
+            value = jnp.sum(
+                jnp.where(lane_ids % TERMS == place, entries, 0.0), axis=1, keepdims=True
+            )
+            value = jnp.broadcast_to(value, (stations, LANES))
+            matrix[k, l] = value + 1.0 if k == l else value
+            place += 1
+    inverse = []
+    ratio = {}
+    for p in range(HARMS):
+        inverse.append(1.0 / matrix[p, p])
+        for k in range(p + 1, HARMS):
+            ratio[k, p] = matrix[k, p] * inverse[p]
+            for l in range(p + 1, k + 1):
+                matrix[k, l] = matrix[k, l] - ratio[k, p] * matrix[l, p]
+
     sums = send_buf[evt, :, 0:USED]
     for j in range(1, evt_count):
         whole(j).wait_recv()
         sums = sums + recv_buf[j - 1, :, 0:USED]
     sum_buf[:, 0:USED] = sums
-
     right = [sum_buf[:, k, :] for k in range(HARMS)]
-    entries = sum_buf[:, HARMS, :]
-    matrix = {}
-    place = 0
-    for k in range(HARMS):
-        for l in range(k + 1):
-            value = jnp.broadcast_to(entries[:, place:place + 1], (stations, LANES))
-            matrix[k, l] = value + 1.0 if k == l else value
-            place += 1
-    inverse = []
     for p in range(HARMS):
-        inverse.append(1.0 / matrix[p, p])
         for k in range(p + 1, HARMS):
-            ratio = matrix[k, p] * inverse[p]
-            for l in range(p + 1, k + 1):
-                matrix[k, l] = matrix[k, l] - ratio * matrix[l, p]
-            right[k] = right[k] - ratio * right[p]
+            right[k] = right[k] - ratio[k, p] * right[p]
     solved = [None] * HARMS
     for k in reversed(range(HARMS)):
-        value = right[k]
+        value = right[k] * inverse[k]
         for l in range(k + 1, HARMS):
-            value = value - matrix[l, k] * solved[l]
-        solved[k] = value * inverse[k]
+            value = value - ratio[l, k] * solved[l]
+        solved[k] = value
         fit_buf[k] = solved[k]
 
     def fits(j):
@@ -276,6 +309,7 @@
             out_ref[t, k, 1:2, :] = row[:, HALF:HALF + share]
     for j in range(1, evt_count):
         whole(j).wait_send()
+        normals(j).wait_send()
     for j in range(1, sta_count):
         fits(j).wait_send()
 
@@ -284,6 +318,7 @@
     _, stations, slots, samples = traces.shape
     depths = depth_index.shape[1]
     share = depths // evt_count
+    pieces = -(-3 * slots // LANES)
     tiles = tile_count(tile_of.shape[0]) // sta_count
     vmem = pl.BlockSpec(memory_space=pltpu.VMEM)
     anywhere = pl.BlockSpec(memory_space=pl.ANY)
@@ -300,8 +335,10 @@
             pltpu.SMEM(counts.shape, jnp.int32),
             pltpu.VMEM(depth_index.shape, jnp.int32),
             pltpu.SMEM(tile_of.shape, jnp.int32),
-            pltpu.VMEM((2 * ROWS, stations, 3 * slots), f32),
-            pltpu.VMEM((stations, LANES), f32),
+            pltpu.VMEM((pieces, 2 * ROWS * stations, LANES), f32),
+            pltpu.VMEM((stations, 4 * ROWS, pieces * LANES), jnp.bfloat16),
+            pltpu.VMEM((ROWS, LANES), f32),
+            pltpu.VMEM((evt_count - 1, ROWS, LANES), f32),
             pltpu.VMEM((evt_count, stations, ROWS, LANES), f32),
             pltpu.VMEM((evt_count - 1, stations, ROWS, LANES), f32),
             pltpu.VMEM((stations, ROWS, LANES), f32),
@@ -309,6 +346,8 @@
             pltpu.VMEM((sta_count - 1, HARMS, stations, LANES), f32),
             pltpu.SemaphoreType.DMA((stations,)),
             pltpu.SemaphoreType.DMA((5,)),
+            pltpu.SemaphoreType.DMA((evt_count - 1,)),
+            pltpu.SemaphoreType.DMA((evt_count - 1,)),
             pltpu.SemaphoreType.DMA((evt_count - 1,)),
             pltpu.SemaphoreType.DMA((evt_count - 1,)),
             pltpu.SemaphoreType.DMA((sta_count - 1,)),

time: 18.4 us -> 18.4 us (level)
  no operation moved by 1% of the time
where the time goes in v3:
time: 18.4 us; the launch traced here: 18.2 us
  Pallas kernels  17.6 us (96%)
  local copies, waits for them, and re-layouts  0.61 us (3%)
    pallas_call x1, Pallas kernels, body(): pl.pallas_call(functools.partial(kernel, evt_count, sta_count, tiles), ou...  17.6 us
    unnamed x1, local copies, waits for them, and re-layouts  0.61 us

profile of v3, /device:TPU:0, one launch (start us, length us, event | category | flops | bytes accessed | tf_op | source)
XLA Modules:
  0.0 18.2 jit_solution(18108599096899918900)
XLA Ops:
  0.0 17.6 %shard_map.64 = f32[4,5,2,64]{3,2,1,0:T(2,128)S(1)} custom-call(bf16[3,8,64,2048]{3,2,1,0:T(8,128)(2,1)} %traces_ref.1, s32[8,64]{1,0:T(8,128)} %baz_hbm.1, s32[8,64]{1,0:T(8,128)} %inc_hbm.1, s32[8]{0:T(128)} %counts_hbm.1, s32[8,512]{1,0:T(8,128)} %depth_hbm.1, s32[32]{0:T(128)} %tile_hbm.1), custom_call_target="tpu_custom_call" | custom-call | tf_op jit(solution)/shard_map/pallas_call | solution.py:326
  17.6 0.6 %copy.8 = f32[4,5,2,64]{3,2,1,0:T(2,128)} copy(f32[4,5,2,64]{3,2,1,0:T(2,128)S(1)} %shard_map.64) | data formatting | bytes 20480

commit v4 on v3

--- a/solution.py
+++ b/solution.py
@@ -15,6 +15,7 @@
 TERMS = 16
 HALF = LANES // 2
 GROUP = 2
+CORES = 2
 
 
 def pick_lanes(values, lanes):
@@ -43,12 +44,16 @@
     normal_buf,
     normal_recv,
     send_buf,
+    pair_buf,
+    relay_buf,
     recv_buf,
     sum_buf,
     fit_buf,
     fit_recv,
     load_sem,
     small_sem,
+    pair_send_sem,
+    pair_recv_sem,
     send_sem,
     recv_sem,
     normal_send_sem,
@@ -62,6 +67,9 @@
     share = depths // evt_count
     evt = lax.axis_index("evt")
     sta = lax.axis_index("sta")
+    z_count = evt_count // CORES
+    z_own = lax.div(evt, CORES)
+    core = lax.rem(evt, CORES)
     f32 = jnp.float32
 
     def load(s):
@@ -158,16 +166,38 @@
             device_id_type=pl.DeviceIdType.MESH,
         )
 
-    def remote(j, s):
-        target = lax.rem(evt + j, evt_count)
+    def to_partner(i):
+        part = pl.ds(i * GROUP, GROUP)
         return pltpu.make_async_remote_copy(
-            src_ref=send_buf.at[target, pl.ds(s, GROUP), 0:USED],
-            dst_ref=recv_buf.at[j - 1, pl.ds(s, GROUP), 0:USED],
+            src_ref=send_buf.at[1 - core, :, part, 0:USED],
+            dst_ref=pair_buf.at[:, part, 0:USED],
+            send_sem=pair_send_sem.at[i],
+            recv_sem=pair_recv_sem.at[i],
+            device_id={"evt": z_own * CORES + 1 - core},
+            device_id_type=pl.DeviceIdType.MESH,
+        )
+
+    def remote(j, first, length):
+        target = lax.rem(z_own + j, z_count)
+        part = pl.ds(first, length)
+        return pltpu.make_async_remote_copy(
+            src_ref=relay_buf.at[target, part, 0:USED],
+            dst_ref=recv_buf.at[j - 1, part, 0:USED],
             send_sem=send_sem.at[j - 1],
             recv_sem=recv_sem.at[j - 1],
-            device_id={"evt": target},
-            device_id_type=pl.DeviceIdType.MESH,
-        )
+            device_id={"evt": target * CORES + core},
+            device_id_type=pl.DeviceIdType.MESH,
+        )
+
+    def forward(i):
+        to_partner(i).wait_recv()
+        part = pl.ds(i * GROUP, GROUP)
+        for z in range(z_count):
+            relay_buf[z, part, 0:USED] = (
+                send_buf[core, z, part, 0:USED] + pair_buf[z, part, 0:USED]
+            )
+        for j in range(1, z_count):
+            remote(j, i * GROUP, GROUP).start()
 
     lane8 = lax.broadcasted_iota(jnp.int32, (ROWS, LANES), 1)
 
@@ -194,7 +224,8 @@
                 left = got[0] if d == 0 else pltpu.roll(got[0], LANES - d * share, 1)
                 move = (HALF - d * share) % LANES
                 rest = got[1] if move == 0 else pltpu.roll(got[1], move, 1)
-                send_buf[z * (LANES // share) + d, s] = jnp.where(lane8 < HALF, left, rest)
+                to = z * (LANES // share) + d
+                send_buf[to % CORES, to // CORES, s] = jnp.where(lane8 < HALF, left, rest)
 
     def step(i, carry):
         at = i * GROUP
@@ -210,21 +241,17 @@
             for j in range(1, evt_count):
                 normals(j).start()
 
-        for j in range(1, evt_count):
-            remote(j, at).start()
+        to_partner(i).start()
+
+        @pl.when(i > 0)
+        def _():
+            forward(i - 1)
+
         return carry
 
-    lax.fori_loop(0, stations // GROUP, step, 0)
-
-    def whole(j):
-        return pltpu.make_async_remote_copy(
-            src_ref=send_buf.at[lax.rem(evt + j, evt_count), :, 0:USED],
-            dst_ref=recv_buf.at[j - 1, :, 0:USED],
-            send_sem=send_sem.at[j - 1],
-            recv_sem=recv_sem.at[j - 1],
-            device_id={"evt": lax.rem(evt + j, evt_count)},
-            device_id_type=pl.DeviceIdType.MESH,
-        )
+    steps = stations // GROUP
+    lax.fori_loop(0, steps, step, 0)
+    forward(steps - 1)
 
     row = normal_buf[0:1]
     for j in range(1, evt_count):
@@ -251,9 +278,9 @@
             for l in range(p + 1, k + 1):
                 matrix[k, l] = matrix[k, l] - ratio[k, p] * matrix[l, p]
 
-    sums = send_buf[evt, :, 0:USED]
-    for j in range(1, evt_count):
-        whole(j).wait_recv()
+    sums = relay_buf[z_own, :, 0:USED]
+    for j in range(1, z_count):
+        remote(j, 0, stations).wait_recv()
         sums = sums + recv_buf[j - 1, :, 0:USED]
     sum_buf[:, 0:USED] = sums
     right = [sum_buf[:, k, :] for k in range(HARMS)]
@@ -308,8 +335,11 @@
             out_ref[t, k, 0:1, :] = row[:, 0:share]
             out_ref[t, k, 1:2, :] = row[:, HALF:HALF + share]
     for j in range(1, evt_count):
-        whole(j).wait_send()
         normals(j).wait_send()
+    for j in range(1, z_count):
+        remote(j, 0, stations).wait_send()
+    for i in range(steps):
+        to_partner(i).wait_send()
     for j in range(1, sta_count):
         fits(j).wait_send()
 
@@ -318,6 +348,7 @@
     _, stations, slots, samples = traces.shape
     depths = depth_index.shape[1]
     share = depths // evt_count
+    z_count = evt_count // CORES
     pieces = -(-3 * slots // LANES)
     tiles = tile_count(tile_of.shape[0]) // sta_count
     vmem = pl.BlockSpec(memory_space=pltpu.VMEM)
@@ -339,15 +370,19 @@
             pltpu.VMEM((stations, 4 * ROWS, pieces * LANES), jnp.bfloat16),
             pltpu.VMEM((ROWS, LANES), f32),
             pltpu.VMEM((evt_count - 1, ROWS, LANES), f32),
-            pltpu.VMEM((evt_count, stations, ROWS, LANES), f32),
-            pltpu.VMEM((evt_count - 1, stations, ROWS, LANES), f32),
+            pltpu.VMEM((CORES, z_count, stations, ROWS, LANES), f32),
+            pltpu.VMEM((z_count, stations, ROWS, LANES), f32),
+            pltpu.VMEM((z_count, stations, ROWS, LANES), f32),
+            pltpu.VMEM((z_count - 1, stations, ROWS, LANES), f32),
             pltpu.VMEM((stations, ROWS, LANES), f32),
             pltpu.VMEM((HARMS, stations, LANES), f32),
             pltpu.VMEM((sta_count - 1, HARMS, stations, LANES), f32),
             pltpu.SemaphoreType.DMA((stations,)),
             pltpu.SemaphoreType.DMA((5,)),
-            pltpu.SemaphoreType.DMA((evt_count - 1,)),
-            pltpu.SemaphoreType.DMA((evt_count - 1,)),
+            pltpu.SemaphoreType.DMA((stations // GROUP,)),
+            pltpu.SemaphoreType.DMA((stations // GROUP,)),
+            pltpu.SemaphoreType.DMA((z_count - 1,)),
+            pltpu.SemaphoreType.DMA((z_count - 1,)),
             pltpu.SemaphoreType.DMA((evt_count - 1,)),
             pltpu.SemaphoreType.DMA((evt_count - 1,)),
             pltpu.SemaphoreType.DMA((sta_count - 1,)),

time: 18.4 us -> 19.3 us (1.049)
  Pallas kernels: 17.6 us -> 18.5 us
    pallas_call x1, Pallas kernels: 17.6 us -> 18.5 us  [body(): pl.pallas_call(functools.partial(kernel, evt_count, sta_count, tiles), ou...]
where the time goes in v4:
time: 19.3 us; the launch traced here: 19.2 us
  Pallas kernels  18.5 us (96%)
  local copies, waits for them, and re-layouts  0.61 us (3%)
    pallas_call x1, Pallas kernels, body(): pl.pallas_call(functools.partial(kernel, evt_count, sta_count, tiles), ou...  18.5 us
    unnamed x1, local copies, waits for them, and re-layouts  0.61 us

profile of v4, /device:TPU:0, one launch (start us, length us, event | category | flops | bytes accessed | tf_op | source)
XLA Modules:
  0.0 19.2 jit_solution(17684438396978576183)
XLA Ops:
  0.0 18.5 %shard_map.64 = f32[4,5,2,64]{3,2,1,0:T(2,128)S(1)} custom-call(bf16[3,8,64,2048]{3,2,1,0:T(8,128)(2,1)} %traces_ref.1, s32[8,64]{1,0:T(8,128)} %baz_hbm.1, s32[8,64]{1,0:T(8,128)} %inc_hbm.1, s32[8]{0:T(128)} %counts_hbm.1, s32[8,512]{1,0:T(8,128)} %depth_hbm.1, s32[32]{0:T(128)} %tile_hbm.1), custom_call_target="tpu_custom_call" | custom-call | tf_op jit(solution)/shard_map/pallas_call | solution.py:357
  18.5 0.6 %copy.8 = f32[4,5,2,64]{3,2,1,0:T(2,128)} copy(f32[4,5,2,64]{3,2,1,0:T(2,128)S(1)} %shard_map.64) | data formatting | bytes 20480

commit v5 on v3

--- a/solution.py
+++ b/solution.py
@@ -14,7 +14,7 @@
 USED = HARMS
 TERMS = 16
 HALF = LANES // 2
-GROUP = 2
+GROUP = 4
 
 
 def pick_lanes(values, lanes):

time: 18.4 us -> 17.8 us (0.967)
  Pallas kernels: 17.6 us -> 17 us
    pallas_call x1, Pallas kernels: 17.6 us -> 17 us  [body(): pl.pallas_call(functools.partial(kernel, evt_count, sta_count, tiles), ou...]
where the time goes in v5:
time: 17.8 us; the launch traced here: 17.7 us
  Pallas kernels  17 us (96%)
  local copies, waits for them, and re-layouts  0.61 us (3%)
    pallas_call x1, Pallas kernels, body(): pl.pallas_call(functools.partial(kernel, evt_count, sta_count, tiles), ou...  17 us
    unnamed x1, local copies, waits for them, and re-layouts  0.61 us

profile of v5, /device:TPU:0, one launch (start us, length us, event | category | flops | bytes accessed | tf_op | source)
XLA Modules:
  0.0 17.7 jit_solution(4251914890141473307)
XLA Ops:
  0.0 17.0 %shard_map.64 = f32[4,5,2,64]{3,2,1,0:T(2,128)S(1)} custom-call(bf16[3,8,64,2048]{3,2,1,0:T(8,128)(2,1)} %traces_ref.1, s32[8,64]{1,0:T(8,128)} %baz_hbm.1, s32[8,64]{1,0:T(8,128)} %inc_hbm.1, s32[8]{0:T(128)} %counts_hbm.1, s32[8,512]{1,0:T(8,128)} %depth_hbm.1, s32[32]{0:T(128)} %tile_hbm.1), custom_call_target="tpu_custom_call" | custom-call | tf_op jit(solution)/shard_map/pallas_call | solution.py:326
  17.0 0.6 %copy.8 = f32[4,5,2,64]{3,2,1,0:T(2,128)} copy(f32[4,5,2,64]{3,2,1,0:T(2,128)S(1)} %shard_map.64) | data formatting | bytes 20480

commit v6 on v5

--- a/solution.py
+++ b/solution.py
@@ -198,9 +198,10 @@
 
     def step(i, carry):
         at = i * GROUP
+        pairs = []
         for g in range(GROUP):
             load(at + g).wait()
-        pairs = [right_sides(at + g) for g in range(GROUP)]
+            pairs.append(right_sides(at + g))
         for g in range(GROUP):
             pick(at + g, pairs[g])
 

time: 17.8 us -> 20 us (1.12)
  Pallas kernels: 17 us -> 19.3 us
    pallas_call x1, Pallas kernels: 17 us -> 19.3 us  [body(): pl.pallas_call(functools.partial(kernel, evt_count, sta_count, tiles), ou...]
where the time goes in v6:
time: 20 us; the launch traced here: 19.9 us
  Pallas kernels  19.3 us (96%)
  local copies, waits for them, and re-layouts  0.61 us (3%)
    pallas_call x1, Pallas kernels, body(): pl.pallas_call(functools.partial(kernel, evt_count, sta_count, tiles), ou...  19.3 us
    unnamed x1, local copies, waits for them, and re-layouts  0.61 us

profile of v6, /device:TPU:0, one launch (start us, length us, event | category | flops | bytes accessed | tf_op | source)
XLA Modules:
  0.0 19.9 jit_solution(4954864871754807563)
XLA Ops:
  0.0 19.3 %shard_map.64 = f32[4,5,2,64]{3,2,1,0:T(2,128)S(1)} custom-call(bf16[3,8,64,2048]{3,2,1,0:T(8,128)(2,1)} %traces_ref.1, s32[8,64]{1,0:T(8,128)} %baz_hbm.1, s32[8,64]{1,0:T(8,128)} %inc_hbm.1, s32[8]{0:T(128)} %counts_hbm.1, s32[8,512]{1,0:T(8,128)} %depth_hbm.1, s32[32]{0:T(128)} %tile_hbm.1), custom_call_target="tpu_custom_call" | custom-call | tf_op jit(solution)/shard_map/pallas_call | solution.py:327
  19.3 0.6 %copy.8 = f32[4,5,2,64]{3,2,1,0:T(2,128)} copy(f32[4,5,2,64]{3,2,1,0:T(2,128)S(1)} %shard_map.64) | data formatting | bytes 20480
